TPU v7x, 32 devices: a whole 2x2x4 slice. The times are simulated.
32 devices in a mesh: groups: 2 (over y), row: 4 (over x, core), col: 4 (over z).
Axes of the slice: x: 2, y: 2, z: 4, core: 2. Of those that a mesh axis runs over, the one named last changes fastest.
Arguments:
- tiles: float32 [512, 128, 128], P(('groups', 'row', 'col')), parts along dimension 0, may hold values from 0 to 9
- tile_index: int32 [512, 2], P(('groups', 'row', 'col')), parts along dimension 0, may hold values from 0 to 3, as said below
- tile_count: int32 [32], P(('groups', 'row', 'col')), parts along dimension 0, may hold values from 4 to 16, as said below
- sources: int32 [16], P('groups'), parts along dimension 0, may hold values from 0 to 2047
Outputs:
- distance: float32 [16, 2048], P('groups', ('row', 'col')), parts along dimension 0
- path_counts: float32 [16, 2048], P('groups', ('row', 'col')), parts along dimension 0
- centrality: float32 [4096], P(('groups', 'row', 'col')), parts along dimension 0
There are 2 independent parts, one for each index of `groups`. A program takes and returns all parts, laid end to end along the dimension named above; each array names one. Nothing has to cross between parts.
Inputs may be any that keep to these rules, and one draw needn't show every extreme that they name: `tile_index`: entry (r, c) of a slot has r below 4 and c below 4; the 16 slots of one device name distinct pairs. `tile_count`: one entry per device; slots of a device from its count on hold only zeros; some device has all 16 slots live.
All inputs are finite; a program needn't handle non-finite values.
Results may differ from a plain program's by a relative error of at most 0.0003.
Values sent between devices are 32-bit elements; how exact they have to be, the bound alone decides.
A program may use at most 64 MiB of HBM per device.

v0:
```python
import jax
import jax.numpy as jnp
from jax import lax
from jax.sharding import PartitionSpec as P

LEVELS = 3
BACK = 2


far_value = 1000000.0
no_edge = 2000000.0


def combined_all(value, axis, join):
    pieces = jax.tree.map(lambda part: lax.all_gather(part, axis), value)
    head = jax.tree.map(lambda part: part[0], pieces)
    tail = jax.tree.map(lambda part: part[1:], pieces)
    running, _ = lax.scan(lambda running, piece: (join(running, piece), None), head, tail)
    return running


def combine_pair(left_pair, right_pair):
    best_dist = jnp.minimum(left_pair[0], right_pair[0])
    total_count = jnp.where(left_pair[0] == best_dist, left_pair[1], 0.0) + jnp.where(
        right_pair[0] == best_dist, right_pair[1], 0.0
    )
    return (best_dist, total_count)


def pick_rows(band, tile_ids, tile_side):
    source_rows = band.shape[0]
    shaped = band.reshape(source_rows, band.shape[1] // tile_side, tile_side)
    return jnp.take(shaped, tile_ids, axis=1).transpose(1, 0, 2)


def split_blocks(values, tile_side):
    block_size = min(16, tile_side)
    blocks = tile_side // block_size
    return values.reshape(values.shape[0], values.shape[1], blocks, block_size).transpose(
        2, 0, 1, 3
    )


def weight_blocks(weights, tile_side):
    block_size = min(16, tile_side)
    blocks = tile_side // block_size
    return weights.reshape(weights.shape[0], blocks, block_size, tile_side).transpose(1, 0, 2, 3)


def relax_group(near_dist, near_count, weights):
    group, source_rows, tile_side = near_dist.shape

    def advance(carried, pieces):
        dist_part, count_part, weight_part = pieces
        reached = dist_part[:, :, :, None] + weight_part[:, None, :, :]
        best_dist = jnp.min(reached, axis=2)
        total_count = jnp.sum(
            jnp.where(reached == best_dist[:, :, None, :], count_part[:, :, :, None], 0.0), axis=2
        )
        return (combine_pair(carried, (best_dist, total_count)), None)

    initial = (
        jnp.full((group, source_rows, tile_side), far_value, jnp.float32),
        jnp.zeros((group, source_rows, tile_side), jnp.float32),
    )
    result, unused = lax.scan(
        advance,
        initial,
        (
            split_blocks(near_dist, tile_side),
            split_blocks(near_count, tile_side),
            weight_blocks(weights, tile_side),
        ),
    )
    return result


def depend_group(upper_dist, lower_dist, lower_coef, weights):
    group, source_rows, tile_side = upper_dist.shape

    def dependency_rows(pieces):
        upper_part, weight_part = pieces
        reached = upper_part[:, :, :, None] + weight_part[:, None, :, :]
        return jnp.sum(
            jnp.where(reached == lower_dist[:, :, None, :], lower_coef[:, :, None, :], 0.0), axis=3
        )

    row_parts = lax.map(
        dependency_rows, (split_blocks(upper_dist, tile_side), weight_blocks(weights, tile_side))
    )
    return row_parts.transpose(1, 2, 0, 3).reshape(group, source_rows, tile_side)


def per_device(tiles, tile_index, tile_count, sources):
    tile_side = tiles.shape[1]
    slot_total = tiles.shape[0]
    source_rows = sources.shape[0]
    row_count = lax.axis_size("row")
    col_count = lax.axis_size("col")
    my_row = lax.axis_index("row")
    my_col = lax.axis_index("col")
    own_ids = (my_row * col_count + my_col) * tile_side + jnp.arange(tile_side, dtype=jnp.int32)
    own_source = own_ids[None, :] == sources[:, None]
    band_ids = my_row * col_count * tile_side + jnp.arange(col_count * tile_side, dtype=jnp.int32)
    band_source = band_ids[None, :] == sources[:, None]
    live_count = tile_count[0]
    start_dist = jnp.where(own_source, 0.0, far_value).astype(jnp.float32)
    source_ones = jnp.where(own_source, 1.0, 0.0).astype(jnp.float32)
    band_dist = jnp.where(band_source, 0.0, far_value).astype(jnp.float32)
    band_paths = jnp.where(band_source, 1.0, 0.0).astype(jnp.float32)

    def group_parts(start, width):
        slot_ids = start + jnp.arange(width, dtype=jnp.int32)
        live = slot_ids < live_count
        weights = jnp.where((tiles > 0) & live[:, None, None], tiles, no_edge)
        return (weights, tile_index, live)

    def run_groups(process, initial):
        return process(0, slot_total, initial)

    def gather_band(dist_part, path_part):
        return (
            lax.all_gather(dist_part, "col", axis=1, tiled=True),
            lax.all_gather(path_part, "col", axis=1, tiled=True),
        )

    column_tiles = jnp.arange(row_count, dtype=jnp.int32)
    row_tiles = jnp.arange(col_count, dtype=jnp.int32)
    own_dist = start_dist
    own_paths = source_ones
    for level_no in range(LEVELS):
        if level_no > 0:
            band_dist, band_paths = gather_band(own_dist, own_paths)

        def forward_group(start, width, carried, band_dist=band_dist, band_paths=band_paths):
            weights, places, live = group_parts(start, width)
            near_dist = pick_rows(band_dist, places[:, 0], tile_side)
            near_count = pick_rows(band_paths, places[:, 0], tile_side)
            found_dist, found_count = relax_group(near_dist, near_count, weights)
            hits = (places[None, :, 1] == column_tiles[:, None]) & live[None, :]
            masked = jnp.where(hits[:, :, None, None], found_dist[None], far_value)
            best_dist = jnp.min(masked, axis=1)
            total_count = jnp.sum(
                jnp.where(
                    hits[:, :, None, None] & (found_dist[None] == best_dist[:, None]),
                    found_count[None],
                    0.0,
                ),
                axis=1,
            )
            return combine_pair(carried, (best_dist, total_count))

        initial = (
            jnp.full((row_count, source_rows, tile_side), far_value, jnp.float32),
            jnp.zeros((row_count, source_rows, tile_side), jnp.float32),
        )
        folded_dist, folded_count = run_groups(forward_group, initial)
        partial_dist = folded_dist.transpose(1, 0, 2).reshape(source_rows, row_count * tile_side)
        partial_count = folded_count.transpose(1, 0, 2).reshape(source_rows, row_count * tile_side)
        merged = combined_all((partial_dist, partial_count), "row", combine_pair)
        found_dist = lax.dynamic_slice_in_dim(merged[0], my_row * tile_side, tile_side, 1)
        found_count = lax.dynamic_slice_in_dim(merged[1], my_row * tile_side, tile_side, 1)
        own_dist = jnp.minimum(start_dist, found_dist)
        own_paths = source_ones + jnp.where(found_dist == own_dist, found_count, 0.0)
    band_dist, band_paths = gather_band(own_dist, own_paths)
    dependency = jnp.zeros((source_rows, tile_side), jnp.float32)
    for back_no in range(BACK):
        coefficient = jnp.where(
            own_paths > 0.5, (1.0 + dependency) / jnp.maximum(own_paths, 1.0), 0.0
        )
        lower_all, coef_all = (
            lax.all_gather(own_dist, "row", axis=1, tiled=True),
            lax.all_gather(coefficient, "row", axis=1, tiled=True),
        )

        def backward_group(start, width, carried, lower_all=lower_all, coef_all=coef_all):
            weights, places, live = group_parts(start, width)
            upper_dist = pick_rows(band_dist, places[:, 0], tile_side)
            lower_dist = pick_rows(lower_all, places[:, 1], tile_side)
            lower_coef = pick_rows(coef_all, places[:, 1], tile_side)
            dep_terms = depend_group(upper_dist, lower_dist, lower_coef, weights)
            hits = (places[None, :, 0] == row_tiles[:, None]) & live[None, :]
            return carried + jnp.sum(
                jnp.where(hits[:, :, None, None], dep_terms[None], 0.0), axis=1
            )

        folded = run_groups(
            backward_group, jnp.zeros((col_count, source_rows, tile_side), jnp.float32)
        )
        accumulated = folded.transpose(1, 0, 2).reshape(source_rows, col_count * tile_side)
        summed = lax.psum_scatter(accumulated, "col", scatter_dimension=1, tiled=True)
        dependency = own_paths * summed
    centrality = jnp.sum(jnp.where(own_source, 0.0, dependency), axis=0) / source_rows
    shown = jnp.where(own_dist < 0.5 * far_value, own_dist, -1.0)
    return (shown, own_paths, centrality)


def solution(mesh):
    in_specs = (
        P(("groups", "row", "col"), None, None),
        P(("groups", "row", "col"), None),
        P(("groups", "row", "col")),
        P("groups"),
    )
    out_specs = (
        P("groups", ("row", "col")),
        P("groups", ("row", "col")),
        P(("groups", "row", "col")),
    )
    return jax.shard_map(
        per_device, mesh=mesh, in_specs=in_specs, out_specs=out_specs, check_vma=False
    )
```

profile of v0, /device:TPU:0, one launch (start us, length us, event | category | flops | bytes accessed | tf_op | source)
XLA Modules:
  0.0 230.2 jit_solution(145529615375615002)
XLA Ops:
  7.2 0.8 compare_and_fusion
  8.0 0.8 slice_bitcast_fusion.6
  8.8 0.7 compare_select_fusion
  12.1 9.8 %while.100 = (s32[]{:T(128)}, f32[16,8,128]{2,1,0:T(8,128)S(1)}, f32[16,8,128]{2,1,0:T(8,128)S(1)}, f32[8,16,8,16]{3,0,2,1:T(8,128)S(1)}, f32[8,16,16,128]{3,2,1...) while((s32[]{:T(128)}, f32[16,8,128]{2,1,0:T(8,128)S(1)}, ...), condition=%wide.region_3.5_spmd.clone, body=%wide.region_0.4_spmd.clone.sunk | while | flops 1671171 | bytes 1171559 | solution.py:66
  22.3 6.2 %all_gather.44 = f32[4,8,512]{2,1,0:T(8,128)S(1)} all-gather(f32[1,8,512]{2,1,0:T(8,128)S(1)} %get-tuple-element.541), channel_id=1, replica_groups=mesh['groups'=2,'row'=4,'col'=4] {'row'}, dimensions={0}, use_global_device_ids=true | all-gather | bytes 81920 | tf_op jit(solution)/shard_map/all_gather | solution.py:15
  29.1 5.5 %all_gather.43 = f32[4,8,512]{2,1,0:T(8,128)S(1)} all-gather(f32[1,8,512]{2,1,0:T(8,128)S(1)} %get-tuple-element.542), channel_id=1, replica_groups=mesh['groups'=2,'row'=4,'col'=4] {'row'}, dimensions={0}, use_global_device_ids=true | all-gather | bytes 81920 | tf_op jit(solution)/shard_map/all_gather | solution.py:15
  34.7 0.8 slice-done
  36.3 13.6 %all_gather.45 = f32[8,512]{1,0:T(8,128)S(1)} all-gather(f32[8,128]{1,0:T(8,128)S(1)} %get-tuple-element.536), channel_id=1, replica_groups=mesh['groups'=2,'row'=4,'col'=4] {'col'}, dimensions={1}, use_global_device_ids=true | all-gather | bytes 20480 | tf_op jit(solution)/shard_map/all_gather | solution.py:123
  50.5 13.2 %all_gather.46 = f32[8,512]{1,0:T(8,128)S(1)} all-gather(f32[8,128]{1,0:T(8,128)S(1)} %get-tuple-element.535), channel_id=1, replica_groups=mesh['groups'=2,'row'=4,'col'=4] {'col'}, dimensions={1}, use_global_device_ids=true | all-gather | bytes 20480 | tf_op jit(solution)/shard_map/all_gather | solution.py:124
  64.7 9.8 %while.101 = (s32[]{:T(128)}, f32[16,8,128]{2,1,0:T(8,128)S(1)}, f32[16,8,128]{2,1,0:T(8,128)S(1)}, f32[8,16,8,16]{3,0,2,1:T(8,128)S(1)}, f32[8,16,16,128]{3,2,1...) while((s32[]{:T(128)}, f32[16,8,128]{2,1,0:T(8,128)S(1)}, ...), condition=%wide.region_11.13_spmd.clone, body=%wide.region_8.12_spmd.clone.sunk | while | flops 1671171 | bytes 1171559 | solution.py:66
  74.8 5.2 %all_gather.48 = f32[4,8,512]{2,1,0:T(8,128)S(1)} all-gather(f32[1,8,512]{2,1,0:T(8,128)S(1)} %get-tuple-element.539), channel_id=1, replica_groups=mesh['groups'=2,'row'=4,'col'=4] {'row'}, dimensions={0}, use_global_device_ids=true | all-gather | bytes 81920 | tf_op jit(solution)/shard_map/all_gather | solution.py:15
  80.7 5.2 %all_gather.47 = f32[4,8,512]{2,1,0:T(8,128)S(1)} all-gather(f32[1,8,512]{2,1,0:T(8,128)S(1)} %get-tuple-element.540), channel_id=1, replica_groups=mesh['groups'=2,'row'=4,'col'=4] {'row'}, dimensions={0}, use_global_device_ids=true | all-gather | bytes 81920 | tf_op jit(solution)/shard_map/all_gather | solution.py:15
  86.0 0.8 slice-done.1
  86.9 13.2 %all_gather.49 = f32[8,512]{1,0:T(8,128)S(1)} all-gather(f32[8,128]{1,0:T(8,128)S(1)} %get-tuple-element.534), channel_id=1, replica_groups=mesh['groups'=2,'row'=4,'col'=4] {'col'}, dimensions={1}, use_global_device_ids=true | all-gather | bytes 20480 | tf_op jit(solution)/shard_map/all_gather | solution.py:123
  100.7 13.2 %all_gather.50 = f32[8,512]{1,0:T(8,128)S(1)} all-gather(f32[8,128]{1,0:T(8,128)S(1)} %get-tuple-element.533), channel_id=1, replica_groups=mesh['groups'=2,'row'=4,'col'=4] {'col'}, dimensions={1}, use_global_device_ids=true | all-gather | bytes 20480 | tf_op jit(solution)/shard_map/all_gather | solution.py:124
  114.9 9.8 %while.102 = (s32[]{:T(128)}, f32[16,8,128]{2,1,0:T(8,128)S(1)}, f32[16,8,128]{2,1,0:T(8,128)S(1)}, f32[8,16,8,16]{3,0,2,1:T(8,128)S(1)}, f32[8,16,16,128]{3,2,1...) while((s32[]{:T(128)}, f32[16,8,128]{2,1,0:T(8,128)S(1)}, ...), condition=%wide.region_19.21_spmd.clone, body=%wide.region_16.20_spmd.clone.sunk | while | flops 1671171 | bytes 1171559 | solution.py:66
  125.0 5.2 %all_gather.52 = f32[4,8,512]{2,1,0:T(8,128)S(1)} all-gather(f32[1,8,512]{2,1,0:T(8,128)S(1)} %get-tuple-element.537), channel_id=1, replica_groups=mesh['groups'=2,'row'=4,'col'=4] {'row'}, dimensions={0}, use_global_device_ids=true | all-gather | bytes 81920 | tf_op jit(solution)/shard_map/all_gather | solution.py:15
  130.9 5.2 %all_gather.51 = f32[4,8,512]{2,1,0:T(8,128)S(1)} all-gather(f32[1,8,512]{2,1,0:T(8,128)S(1)} %get-tuple-element.538), channel_id=1, replica_groups=mesh['groups'=2,'row'=4,'col'=4] {'row'}, dimensions={0}, use_global_device_ids=true | all-gather | bytes 81920 | tf_op jit(solution)/shard_map/all_gather | solution.py:15
  136.1 0.8 slice-done.2
  137.1 13.2 %all_gather.53 = f32[8,512]{1,0:T(8,128)S(1)} all-gather(f32[8,128]{1,0:T(8,128)S(1)} %get-tuple-element.522), channel_id=1, replica_groups=mesh['groups'=2,'row'=4,'col'=4] {'col'}, dimensions={1}, use_global_device_ids=true | all-gather | bytes 20480 | tf_op jit(solution)/shard_map/all_gather | solution.py:123
  150.3 5.2 %all_gather.54 = f32[8,512]{1,0:T(8,128)S(1)} all-gather(f32[8,128]{1,0:T(8,128)S(1)} %get-tuple-element.522), channel_id=1, replica_groups=mesh['groups'=2,'row'=4,'col'=4] {'row'}, dimensions={1}, use_global_device_ids=true | all-gather | bytes 20480 | tf_op jit(solution)/shard_map/all_gather | solution.py:172
  156.1 5.2 %all_gather.55 = f32[8,512]{1,0:T(8,128)S(1)} all-gather(f32[8,128]{1,0:T(8,128)S(1)} %get-tuple-element.520), channel_id=1, replica_groups=mesh['groups'=2,'row'=4,'col'=4] {'row'}, dimensions={1}, use_global_device_ids=true | all-gather | bytes 20480 | tf_op jit(solution)/shard_map/all_gather | solution.py:173
  162.9 6.1 %while.98 = (s32[]{:T(128)}, f32[8,16,8,16]{3,2,1,0:T(8,128)S(1)}, f32[8,16,8,16]{3,2,1,0:T(8,128)S(1)}, f32[8,16,16,128]{3,2,1,0:T(8,128)S(1)}, f32[16,8,128]{2...) while((s32[]{:T(128)}, f32[8,16,8,16]{3,2,1,0:T(8,128)S(1)}, f32[8,16,8,16]{3,2,1,0:T(8,128)S(1)}, ...), condition=%wide.region_26.28_spmd, body=%wide.region_24.27_spmd.sunk | while | flops 1046530 | bytes 688217 | solution.py:88
  163.7 0.7 select_reduce_fusion.18
  165.2 0.7 select_reduce_fusion.18
  169.5 0.7 select_reduce_fusion.6
  170.3 20.4 %reduce-scatter.3.cloned.1.call-done = f32[8,128]{1,0:T(8,128)} async-done(((f32[8,512]{1,0:T(8,128)}), f32[8,128]{1,0:T(8,128)}) %reduce-scatter.3.cloned.1.call-update) | async-done | bytes 4112 | tf_op jit(solution)/shard_map/reduce_scatter | solution.py:191
  191.3 5.2 %all_gather.56 = f32[8,512]{1,0:T(8,128)S(1)} all-gather(f32[8,128]{1,0:T(8,128)S(1)} %divide_select_fusion), channel_id=1, replica_groups=mesh['groups'=2,'row'=4,'col'=4] {'row'}, dimensions={1}, use_global_device_ids=true | all-gather | bytes 20480 | tf_op jit(solution)/shard_map/all_gather | solution.py:173
  197.2 6.1 %while.99 = (s32[]{:T(128)}, f32[8,16,8,16]{3,2,1,0:T(8,128)S(1)}, f32[8,16,8,16]{3,2,1,0:T(8,128)S(1)}, f32[8,16,16,128]{3,2,1,0:T(8,128)S(1)}, f32[16,8,128]{2...) while((s32[]{:T(128)}, f32[8,16,8,16]{3,2,1,0:T(8,128)S(1)}, f32[8,16,8,16]{3,2,1,0:T(8,128)S(1)}, ...), condition=%wide.region_31.33_spmd, body=%wide.region_29.32_spmd.sunk | while | flops 1046530 | bytes 688217 | solution.py:88
  203.9 0.7 select_reduce_fusion.5
  205.2 16.9 %reduce-scatter.5.cloned.1.call-done = f32[8,128]{1,0:T(8,128)} async-done(((f32[8,512]{1,0:T(8,128)}), f32[8,128]{1,0:T(8,128)}) %reduce-scatter.5.cloned.1.call-update) | async-done | bytes 4112 | tf_op jit(solution)/shard_map/reduce_scatter | solution.py:191
  222.1 0.8 fusion.12
  (280 shorter events, 53.1 us)
Async XLA Ops:
  7.2 4.7 %copy-start = (f32[16,128,128]{2,1,0:T(8,128)S(1)}, f32[16,128,128]{2,1,0:T(8,128)}, u32[]{:S(2)}) copy-start(f32[16,128,128]{2,1,0:T(8,128)} %param.22) | copy-start | bytes 3145732
  7.2 183.5 %reduce-scatter.3.cloned.1.call-start = ((), (), s32[]{:S(2)}) async-start(), calls=%async_computation.2 | async-start | bytes 20480 | tf_op jit(solution)/shard_map/reduce_scatter | solution.py:191
  28.5 0.6 copy-start.1
  34.6 0.8 slice-start
  35.5 0.7 copy-start.5
  80.1 0.6 copy-start.2
  85.9 0.8 slice-start.1
  130.3 0.6 copy-start.3
  136.1 0.8 slice-start.2
  137.1 85.0 %copy-start.4 = (f32[8,128]{1,0:T(8,128)}, f32[8,128]{1,0:T(8,128)S(1)}, u32[]{:S(2)}) copy-start(f32[8,128]{1,0:T(8,128)S(1)} %get-tuple-element.521) | copy-start | bytes 12292
  170.3 51.9 %reduce-scatter.5.cloned.1.call-start = ((), (), s32[]{:S(2)}) async-start(), calls=%async_computation.3 | async-start | bytes 20480 | tf_op jit(solution)/shard_map/reduce_scatter | solution.py:191
Sparse Core Ops, SparseCore 0:
  170.4 20.2 reduce-scatter.2
  204.7 17.3 reduce-scatter.4
where the time goes:
time: 231 us; the launch traced here: 230 us
  blocking collectives  115 us (50%)
  other arithmetic  43.7 us (19%)
  waiting for transfers between devices  37.3 us (16%)
  local copies, waits for them, and re-layouts  17.2 us (7%)
  between operations  15.2 us (7%)
    all_gather x3, blocking collectives, gather_band(): lax.all_gather(dist_part, 'col', axis=1, tiled=True)  40 us
    reduce_scatter x2, waiting for transfers between devices, per_device(): lax.psum_scatter(accumulated, 'col', scatter_dimension=1, tiled=True)  37.3 us
    all_gather x6, blocking collectives, combined_all(): pieces = jax.tree.map(lambda part: lax.all_gather(part, axis), value)  32.6 us
    all_gather x2, blocking collectives, gather_band(): lax.all_gather(path_part, 'col', axis=1, tiled=True)  26.4 us
    reduce_sum x24, other arithmetic, advance(): jnp.sum(jnp.where(reached == best_dist[:, :, None, :], count_part[:, :, :...  14.9 us
    reduce_sum x16, other arithmetic, dependency_rows(): jnp.sum(jnp.where(reached == lower_dist[:, :, None, :], lower_coef[:, :,...  10.9 us
    all_gather x2, blocking collectives, per_device(): lax.all_gather(coefficient, 'row', axis=1, tiled=True)  10.4 us
    reduce_min x24, other arithmetic, advance(): best_dist = jnp.min(reached, axis=2)  9.06 us
  transfers between devices with their start and end apart: 2, of which 2 were waited for; matrix products, arithmetic and copies ran while one was open for 0% of the time, Pallas kernels for 0%

commit v1 on v0

v1 whole, which is shorter than its diff:
```python
import functools

import jax
import jax.numpy as jnp
from jax import lax
from jax.experimental import pallas as pl
from jax.experimental.pallas import tpu as pltpu
from jax.sharding import PartitionSpec as P

LEVELS = 3
BACK = 2
CHUNK = 4

far_value = 1000000.0
no_edge = 2000000.0
half_far = 500000.0


def partner(me, step, count):
    if count & (count - 1):
        return (me + step) % count
    total = 0
    bit = 1
    while bit < count:
        total = total + ((me // bit) % 2 + (step // bit) % 2) % 2 * bit
        bit *= 2
    return total


def body(
    row_count,
    col_count,
    index_ref,
    count_ref,
    source_ref,
    tiles_ref,
    dist_out,
    path_out,
    cent_out,
    raw,
    place_ref,
    weights,
    weights_back,
    partial,
    merged,
    band,
    lower,
    sums_out,
    sums_in,
    load_sem,
    row_send,
    row_recv,
    col_send,
    col_recv,
):
    slot_total, tile_side = raw.shape[0], raw.shape[1]
    source_rows = dist_out.shape[0]
    my_row = lax.axis_index("row")
    my_col = lax.axis_index("col")
    positions = row_count * col_count
    row_chunk = CHUNK if row_count % CHUNK == 0 else 1
    col_chunk = CHUNK if col_count % CHUNK == 0 else 1
    wide = (source_rows, tile_side)
    pending = []

    load = pltpu.make_async_copy(tiles_ref, raw, load_sem)
    load.start()
    barrier = pltpu.get_barrier_semaphore()
    for axis, me, count in (("row", my_row, row_count), ("col", my_col, col_count)):
        for step in range(1, count):
            pl.semaphore_signal(
                barrier,
                inc=1,
                device_id={axis: partner(me, step, count)},
                device_id_type=pl.DeviceIdType.MESH,
            )

    def push(axis, stage, source_of, target):
        me, count = (my_row, row_count) if axis == "row" else (my_col, col_count)
        send, recv = (row_send, row_recv) if axis == "row" else (col_send, col_recv)
        for step in range(1, count):
            other = partner(me, step, count)
            copy = pltpu.make_async_remote_copy(
                src_ref=source_of(other),
                dst_ref=target,
                send_sem=send.at[stage, step],
                recv_sem=recv.at[stage, me],
                device_id={axis: other},
                device_id_type=pl.DeviceIdType.MESH,
            )
            copy.start()
            pending.append(copy)

    def arrived(axis, stage, other, target):
        send, recv = (row_send, row_recv) if axis == "row" else (col_send, col_recv)
        pltpu.make_async_remote_copy(
            src_ref=target,
            dst_ref=target,
            send_sem=send.at[stage, 0],
            recv_sem=recv.at[stage, other],
            device_id={axis: other},
            device_id_type=pl.DeviceIdType.MESH,
        ).wait_recv()

    live_count = count_ref[0]

    def find_slot(position, carried):
        found = jnp.int32(-1)
        for slot in range(slot_total):
            here = (index_ref[slot, 0] * row_count + index_ref[slot, 1] == position) & (
                slot < live_count
            )
            found = jnp.where(here, jnp.int32(slot), found)
        place_ref[position] = found
        return carried

    lax.fori_loop(0, positions, find_slot, 0)

    lane = lax.broadcasted_iota(jnp.int32, wide, 1)
    sub = lax.broadcasted_iota(jnp.int32, wide, 0)
    own_base = (my_row * col_count + my_col) * tile_side
    wanted = jnp.full(wide, -1, jnp.int32)
    for row in range(source_rows):
        wanted = jnp.where(sub == row, source_ref[row] - own_base, wanted)
    own_source = lane == wanted
    start_dist = jnp.where(own_source, 0.0, far_value).astype(jnp.float32)
    source_ones = jnp.where(own_source, 1.0, 0.0).astype(jnp.float32)

    load.wait()

    def prepare(position, carried):
        slot = place_ref[position]
        tile = raw[jnp.maximum(slot, 0)]
        limit = jnp.where(slot >= 0, 0.0, far_value).astype(jnp.float32)
        weights[position] = jnp.where(tile > limit, tile, no_edge)
        return carried

    lax.fori_loop(0, positions, prepare, 0)

    band_base = my_row * col_count * tile_side

    def first_level(column, carried):
        best = jnp.full(wide, far_value, jnp.float32)
        for row in range(source_rows):
            place = source_ref[row] - band_base
            inside = (place >= 0) & (place < col_count * tile_side)
            place = jnp.clip(place, 0, col_count * tile_side - 1)
            line = weights[
                (place // tile_side) * row_count + column, pl.ds(place % tile_side, 1), :
            ]
            limit = jnp.where(inside, no_edge, 0.0).astype(jnp.float32)
            best = jnp.where((sub == row) & (line < limit), line, best)
        partial[0, column, 0] = best
        return carried

    lax.fori_loop(0, row_count, first_level, 0)
    pl.semaphore_wait(barrier, row_count + col_count - 2)

    push("row", 0, lambda other: partial.at[0, other, 0], merged.at[0, my_row, 0])
    found_dist = partial[0, my_row, 0]
    for step in range(1, row_count):
        other = partner(my_row, step, row_count)
        arrived("row", 0, other, merged.at[0, other, 0])
        found_dist = jnp.minimum(found_dist, merged[0, other, 0])
    own_dist = jnp.minimum(start_dist, found_dist)
    own_paths = None
    band[0, my_col, 0] = own_dist
    push("col", 0, lambda other: band.at[0, my_col, 0], band.at[0, my_col, 0])

    def turn(position, carried):
        weights_back[position] = weights[position].T
        return carried

    def forward(level):
        near = band.at[level - 1]
        best_ref = partial.at[level]

        def clear(column, carried):
            best_ref[column, 0] = jnp.full(wide, far_value, jnp.float32)
            best_ref[column, 1] = jnp.zeros(wide, jnp.float32)
            return carried

        lax.fori_loop(0, row_count, clear, 0)

        def from_block(step, carried):
            block = partner(my_col, step, col_count)

            @pl.when(step > 0)
            def _():
                if level == 1:
                    arrived("col", 0, block, band.at[0, block, 0])
                else:
                    arrived("col", level - 1, block, band.at[level - 1, block])

            near_dist = near[block, 0]
            if level == 1:
                near_count = jnp.where(near_dist < half_far, 1.0, 0.0).astype(jnp.float32)
            else:
                near_count = near[block, 1]

            def columns(group, carried):
                first = group * row_chunk
                place = block * row_count + first
                before = [best_ref[first + t, 0] for t in range(row_chunk)]
                best = list(before)
                for u in range(tile_side):
                    wide_dist = jnp.broadcast_to(near_dist[:, u : u + 1], wide)
                    for t in range(row_chunk):
                        line = weights[place + t, u : u + 1, :]
                        best[t] = jnp.minimum(best[t], wide_dist + line)
                total = [
                    jnp.where(before[t] == best[t], best_ref[first + t, 1], 0.0)
                    for t in range(row_chunk)
                ]
                for u in range(tile_side):
                    wide_dist = jnp.broadcast_to(near_dist[:, u : u + 1], wide)
                    wide_count = jnp.broadcast_to(near_count[:, u : u + 1], wide)
                    for t in range(row_chunk):
                        line = weights[place + t, u : u + 1, :]
                        total[t] += jnp.where(wide_dist + line == best[t], wide_count, 0.0)
                for t in range(row_chunk):
                    best_ref[first + t, 0] = best[t]
                    best_ref[first + t, 1] = total[t]
                return carried

            return lax.fori_loop(0, row_count // row_chunk, columns, carried)

        lax.fori_loop(0, col_count, from_block, 0)
        push("row", level, lambda other: best_ref.at[other], merged.at[level, my_row])
        found_dist = best_ref[my_row, 0]
        found_count = best_ref[my_row, 1]
        for step in range(1, row_count):
            other = partner(my_row, step, row_count)
            arrived("row", level, other, merged.at[level, other])
            other_dist = merged[level, other, 0]
            both = jnp.minimum(found_dist, other_dist)
            found_count = jnp.where(found_dist == both, found_count, 0.0) + jnp.where(
                other_dist == both, merged[level, other, 1], 0.0
            )
            found_dist = both
        own_dist = jnp.minimum(start_dist, found_dist)
        own_paths = source_ones + jnp.where(found_dist == own_dist, found_count, 0.0)
        return own_dist, own_paths

    lax.fori_loop(0, positions, turn, 0)
    for level in range(1, LEVELS):
        own_dist, own_paths = forward(level)
        if level < LEVELS - 1:
            band[level, my_col, 0] = own_dist
            band[level, my_col, 1] = own_paths
            push("col", level, lambda other: band.at[level, my_col], band.at[level, my_col])

    last = LEVELS - 1
    dependency = jnp.zeros(wide, jnp.float32)
    for back in range(BACK):
        coefficient = jnp.where(
            own_paths > 0.5, (1.0 + dependency) / jnp.maximum(own_paths, 1.0), 0.0
        )
        if back == 0:
            band[last, my_col, 0] = own_dist
            push("col", last, lambda other: band.at[last, my_col, 0], band.at[last, my_col, 0])
            lower[0, my_row, 0] = own_dist
            lower[0, my_row, 1] = coefficient
            push("row", LEVELS, lambda other: lower.at[0, my_row], lower.at[0, my_row])
            dist_out[...] = jnp.where(own_dist < half_far, own_dist, -1.0)
            path_out[...] = own_paths
        else:
            lower[back, my_row, 1] = coefficient
            push(
                "row",
                LEVELS + back,
                lambda other: lower.at[back, my_row, 1],
                lower.at[back, my_row, 1],
            )

        def clear(block, carried):
            sums_out[back, block] = jnp.zeros(wide, jnp.float32)
            return carried

        lax.fori_loop(0, col_count, clear, 0)
        if back == 0:
            for step in range(1, col_count):
                other = partner(my_col, step, col_count)
                arrived("col", last, other, band.at[last, other, 0])

        def from_column(step, carried):
            column = partner(my_row, step, row_count)

            @pl.when(step > 0)
            def _():
                if back == 0:
                    arrived("row", LEVELS, column, lower.at[0, column])
                else:
                    arrived("row", LEVELS + back, column, lower.at[back, column, 1])

            low_dist = lower[0, column, 0]
            low_coef = lower[back, column, 1]

            def blocks(group, carried):
                first = group * col_chunk
                upper = [band[last, first + t, 0] for t in range(col_chunk)]
                total = [sums_out[back, first + t] for t in range(col_chunk)]
                for v in range(tile_side):
                    wide_dist = jnp.broadcast_to(low_dist[:, v : v + 1], wide)
                    wide_coef = jnp.broadcast_to(low_coef[:, v : v + 1], wide)
                    for t in range(col_chunk):
                        line = weights_back[(first + t) * row_count + column, v : v + 1, :]
                        total[t] += jnp.where(upper[t] + line == wide_dist, wide_coef, 0.0)
                for t in range(col_chunk):
                    sums_out[back, first + t] = total[t]
                return carried

            return lax.fori_loop(0, col_count // col_chunk, blocks, carried)

        lax.fori_loop(0, row_count, from_column, 0)
        stage = LEVELS + back
        push("col", stage, lambda other: sums_out.at[back, other], sums_in.at[back, my_col])
        summed = sums_out[back, my_col]
        for step in range(1, col_count):
            other = partner(my_col, step, col_count)
            arrived("col", stage, other, sums_in.at[back, other])
            summed += sums_in[back, other]
        dependency = own_paths * summed
    cent_out[...] = (
        jnp.sum(jnp.where(own_source, 0.0, dependency), axis=0, keepdims=True) / source_rows
    )
    for copy in pending:
        copy.wait_send()


def solution(mesh):
    row_count = mesh.shape["row"]
    col_count = mesh.shape["col"]
    stages = LEVELS + BACK

    def per_device(tiles, tile_index, tile_count, sources):
        slot_total, tile_side = tiles.shape[0], tiles.shape[1]
        source_rows = sources.shape[0]
        wide = (source_rows, tile_side)
        positions = row_count * col_count
        vector = pl.BlockSpec(memory_space=pltpu.VMEM)
        scalar = pl.BlockSpec(memory_space=pltpu.SMEM)
        distance, paths, centrality = pl.pallas_call(
            functools.partial(body, row_count, col_count),
            out_shape=(
                jax.ShapeDtypeStruct(wide, jnp.float32),
                jax.ShapeDtypeStruct(wide, jnp.float32),
                jax.ShapeDtypeStruct((1, tile_side), jnp.float32),
            ),
            in_specs=[scalar, scalar, scalar, pl.BlockSpec(memory_space=pl.ANY)],
            out_specs=(vector, vector, vector),
            scratch_shapes=[
                pltpu.VMEM((slot_total, tile_side, tile_side), jnp.float32),
                pltpu.SMEM((positions,), jnp.int32),
                pltpu.VMEM((positions, tile_side, tile_side), jnp.float32),
                pltpu.VMEM((positions, tile_side, tile_side), jnp.float32),
                pltpu.VMEM((LEVELS, row_count, 2) + wide, jnp.float32),
                pltpu.VMEM((LEVELS, row_count, 2) + wide, jnp.float32),
                pltpu.VMEM((LEVELS, col_count, 2) + wide, jnp.float32),
                pltpu.VMEM((BACK, row_count, 2) + wide, jnp.float32),
                pltpu.VMEM((BACK, col_count) + wide, jnp.float32),
                pltpu.VMEM((BACK, col_count) + wide, jnp.float32),
                pltpu.SemaphoreType.DMA,
                pltpu.SemaphoreType.DMA((stages, row_count)),
                pltpu.SemaphoreType.DMA((stages, row_count)),
                pltpu.SemaphoreType.DMA((stages, col_count)),
                pltpu.SemaphoreType.DMA((stages, col_count)),
            ],
            compiler_params=pltpu.CompilerParams(
                collective_id=0,
                has_side_effects=True,
            ),
        )(tile_index, tile_count, sources, tiles)
        return distance, paths, centrality.reshape(tile_side)

    in_specs = (
        P(("groups", "row", "col"), None, None),
        P(("groups", "row", "col"), None),
        P(("groups", "row", "col")),
        P("groups"),
    )
    out_specs = (
        P("groups", ("row", "col")),
        P("groups", ("row", "col")),
        P(("groups", "row", "col")),
    )
    return jax.shard_map(
        per_device, mesh=mesh, in_specs=in_specs, out_specs=out_specs, check_vma=False
    )
```

time: 231 us -> 45 us (0.19)
  blocking collectives: 115 us -> 0 us
  other arithmetic: 43.7 us -> 0 us
  Pallas kernels: 0 us -> 40.2 us
  waiting for transfers between devices: 37.3 us -> 0 us
  local copies, waits for them, and re-layouts: 17.2 us -> 3.16 us
  between operations: 15.2 us -> 1.32 us
    all_gather x14 -> x0, blocking collectives: 115 us -> none  [the longest x3 40 us: gather_band(): lax.all_gather(dist_part, 'col', axis=1, tiled=True)]
    pallas_call x0 -> x1, Pallas kernels: none -> 40.2 us  [per_device(): pl.pallas_call(functools.partial(body, row_count, col_count), out_shape=(...]
    reduce_scatter x2 -> x0, waiting for transfers between devices: 37.3 us -> none  [per_device(): lax.psum_scatter(accumulated, 'col', scatter_dimension=1, tiled=True)]
    reduce_sum x46 -> x0, other arithmetic: 28.4 us -> none  [the longest x24 14.9 us: advance(): jnp.sum(jnp.where(reached == best_dist[:, :, None, :], count_part[:, :, :...]
    reduce_min x27 -> x0, other arithmetic: 9.46 us -> none  [the longest x24 9.06 us: advance(): best_dist = jnp.min(reached, axis=2)]
    gather x10 -> x0, local copies, waits for them, and re-layouts: 5.64 us -> none  [pick_rows(): return jnp.take(shaped, tile_ids, axis=1).transpose(1, 0, 2)]
    select_n x10 -> x0, other arithmetic: 2.74 us -> none  [the longest x2 0.76 us: per_device(): jnp.where(own_paths > 0.5, (1.0 + dependency) / jnp.maximum(own_paths, 1....]
    dynamic_slice x24 -> x0, local copies, waits for them, and re-layouts: 2.37 us -> none  [relax_group(): lax.scan(advance, initial, (split_blocks(near_dist, tile_side), split_blo...]
  transfers between devices with their start and end apart: 2 -> 0, of which waited for: 2 -> 0; matrix products, arithmetic and copies ran while one was open for 0% -> 0% of each run, Pallas kernels for 0% -> 0%
where the time goes in v1:
time: 45 us; the launch traced here: 44.7 us
  Pallas kernels  40.2 us (89%)
  local copies, waits for them, and re-layouts  3.16 us (7%)
  between operations  1.32 us (3%)
    pallas_call x1, Pallas kernels, per_device(): pl.pallas_call(functools.partial(body, row_count, col_count), out_shape=(...  40.2 us
    unnamed x12, local copies, waits for them, and re-layouts  3.16 us

profile of v1, /device:TPU:0, one launch (start us, length us, event | category | flops | bytes accessed | tf_op | source)
XLA Modules:
  0.0 44.7 jit_solution(16122635803301935206)
XLA Ops:
  0.6 0.0 copy-start.2
  1.3 0.0 copy-done.2
  1.3 0.7 %copy.7.index_ref = s32[16,2]{1,0:T(8,128)} copy(s32[16,2]{0,1:T(2,128)S(1)} %copy-done.2) | data formatting | bytes 256 | tf_op args[1]
  2.0 40.2 %shard_map.67 = (f32[8,128]{1,0:T(8,128)}, f32[8,128]{1,0:T(8,128)}, f32[1,128]{1,0:T(1,128)}) custom-call(s32[16,2]{1,0:T(8,128)} %copy.7.index_ref, s32[1]{0:T(128)S(6)} %copy.11.count_ref, s32[8]{0:T(128)} %source_ref.1, f32[16,128,128]{2,1,0:T(8,128)} %tiles_ref.1), custom_call_target="tpu_custom_call" | custom-call | tf_op jit(solution)/shard_map/pallas_call | solution.py:343
  42.2 0.0 copy-start.1
  42.3 0.7 %copy-done.1 = f32[8,128]{1,0:T(8,128)S(1)} copy-done((f32[8,128]{1,0:T(8,128)S(1)}, f32[8,128]{1,0:T(8,128)}, u32[]{:S(2)}) %copy-start.1) | copy-done | bytes 4120
  42.9 0.0 copy-start
  42.9 0.6 %copy.12 = f32[8,128]{1,0:T(8,128)} copy(f32[8,128]{1,0:T(8,128)S(1)} %copy-done.1) | data formatting | bytes 8192
  43.5 0.1 copy-done
  43.6 0.0 copy-start.3
  43.6 0.6 %copy.13 = f32[8,128]{1,0:T(8,128)} copy(f32[8,128]{1,0:T(8,128)S(1)} %copy-done) | data formatting | bytes 8192
  44.2 0.0 copy-done.3
  44.2 0.5 %copy.14 = f32[128]{0:T(128)} copy(f32[128]{0:T(128)S(1)} %bitcast.1) | data formatting | bytes 1024
Async XLA Ops:
  0.6 0.7 %copy-start.2 = (s32[16,2]{0,1:T(2,128)S(1)}, s32[16,2]{0,1:T(2,128)}, u32[]{:S(2)}) copy-start(s32[16,2]{0,1:T(2,128)} %param.5) | copy-start | bytes 388
  42.2 0.7 %copy-start.1 = (f32[8,128]{1,0:T(8,128)S(1)}, f32[8,128]{1,0:T(8,128)}, u32[]{:S(2)}) copy-start(f32[8,128]{1,0:T(8,128)} %get-tuple-element.12) | copy-start | bytes 12292
  42.9 0.7 %copy-start = (f32[8,128]{1,0:T(8,128)S(1)}, f32[8,128]{1,0:T(8,128)}, u32[]{:S(2)}) copy-start(f32[8,128]{1,0:T(8,128)} %get-tuple-element.13) | copy-start | bytes 12292
  43.6 0.6 %copy-start.3 = (f32[1,128]{1,0:T(1,128)S(1)}, f32[1,128]{1,0:T(1,128)}, u32[]{:S(2)}) copy-start(f32[1,128]{1,0:T(1,128)} %get-tuple-element.8) | copy-start | bytes 1540

commit v2 on v1

--- a/solution.py
+++ b/solution.py
@@ -34,9 +34,7 @@
     count_ref,
     source_ref,
     tiles_ref,
-    dist_out,
-    path_out,
-    cent_out,
+    packed,
     raw,
     place_ref,
     weights,
@@ -54,7 +52,7 @@
     col_recv,
 ):
     slot_total, tile_side = raw.shape[0], raw.shape[1]
-    source_rows = dist_out.shape[0]
+    source_rows = source_ref.shape[0]
     my_row = lax.axis_index("row")
     my_col = lax.axis_index("col")
     positions = row_count * col_count
@@ -78,7 +76,7 @@
     def push(axis, stage, source_of, target):
         me, count = (my_row, row_count) if axis == "row" else (my_col, col_count)
         send, recv = (row_send, row_recv) if axis == "row" else (col_send, col_recv)
-        for step in range(1, count):
+        for step in reversed(range(1, count)):
             other = partner(me, step, count)
             copy = pltpu.make_async_remote_copy(
                 src_ref=source_of(other),
@@ -103,14 +101,15 @@
         ).wait_recv()
 
     live_count = count_ref[0]
+    holds = []
+    for slot in range(slot_total):
+        position = index_ref[0, slot] * row_count + index_ref[1, slot]
+        holds.append(jnp.where(slot < live_count, position, -1))
 
     def find_slot(position, carried):
         found = jnp.int32(-1)
         for slot in range(slot_total):
-            here = (index_ref[slot, 0] * row_count + index_ref[slot, 1] == position) & (
-                slot < live_count
-            )
-            found = jnp.where(here, jnp.int32(slot), found)
+            found = jnp.where(holds[slot] == position, jnp.int32(slot), found)
         place_ref[position] = found
         return carried
 
@@ -128,6 +127,25 @@
 
     load.wait()
 
+    band_base = my_row * col_count * tile_side
+
+    def first_level(column, carried):
+        best = jnp.full(wide, far_value, jnp.float32)
+        for row in range(source_rows):
+            place = source_ref[row] - band_base
+            inside = (place >= 0) & (place < col_count * tile_side)
+            place = jnp.clip(place, 0, col_count * tile_side - 1)
+            slot = place_ref[(place // tile_side) * row_count + column]
+            line = raw[jnp.maximum(slot, 0), pl.ds(place % tile_side, 1), :]
+            limit = jnp.where(inside & (slot >= 0), 0.0, far_value).astype(jnp.float32)
+            best = jnp.where((sub == row) & (line > limit), line, best)
+        partial[0, column, 0] = best
+        return carried
+
+    lax.fori_loop(0, row_count, first_level, 0)
+    pl.semaphore_wait(barrier, row_count + col_count - 2)
+
+    push("row", 0, lambda other: partial.at[0, other, 0], merged.at[0, my_row, 0])
     def prepare(position, carried):
         slot = place_ref[position]
         tile = raw[jnp.maximum(slot, 0)]
@@ -137,26 +155,6 @@
 
     lax.fori_loop(0, positions, prepare, 0)
 
-    band_base = my_row * col_count * tile_side
-
-    def first_level(column, carried):
-        best = jnp.full(wide, far_value, jnp.float32)
-        for row in range(source_rows):
-            place = source_ref[row] - band_base
-            inside = (place >= 0) & (place < col_count * tile_side)
-            place = jnp.clip(place, 0, col_count * tile_side - 1)
-            line = weights[
-                (place // tile_side) * row_count + column, pl.ds(place % tile_side, 1), :
-            ]
-            limit = jnp.where(inside, no_edge, 0.0).astype(jnp.float32)
-            best = jnp.where((sub == row) & (line < limit), line, best)
-        partial[0, column, 0] = best
-        return carried
-
-    lax.fori_loop(0, row_count, first_level, 0)
-    pl.semaphore_wait(barrier, row_count + col_count - 2)
-
-    push("row", 0, lambda other: partial.at[0, other, 0], merged.at[0, my_row, 0])
     found_dist = partial[0, my_row, 0]
     for step in range(1, row_count):
         other = partner(my_row, step, row_count)
@@ -262,8 +260,8 @@
             lower[0, my_row, 0] = own_dist
             lower[0, my_row, 1] = coefficient
             push("row", LEVELS, lambda other: lower.at[0, my_row], lower.at[0, my_row])
-            dist_out[...] = jnp.where(own_dist < half_far, own_dist, -1.0)
-            path_out[...] = own_paths
+            packed[0] = jnp.where(own_dist < half_far, own_dist, -1.0)
+            packed[1] = own_paths
         else:
             lower[back, my_row, 1] = coefficient
             push(
@@ -277,42 +275,70 @@
             sums_out[back, block] = jnp.zeros(wide, jnp.float32)
             return carried
 
-        lax.fori_loop(0, col_count, clear, 0)
         if back == 0:
-            for step in range(1, col_count):
-                other = partner(my_col, step, col_count)
-                arrived("col", last, other, band.at[last, other, 0])
-
-        def from_column(step, carried):
-            column = partner(my_row, step, row_count)
-
-            @pl.when(step > 0)
-            def _():
-                if back == 0:
-                    arrived("row", LEVELS, column, lower.at[0, column])
-                else:
+            for step in range(1, row_count):
+                other = partner(my_row, step, row_count)
+                arrived("row", LEVELS, other, lower.at[0, other])
+
+            def from_block(step, carried):
+                block = partner(my_col, step, col_count)
+
+                @pl.when(step > 0)
+                def _():
+                    arrived("col", last, block, band.at[last, block, 0])
+
+                upper = band[last, block, 0]
+
+                def columns(group, total):
+                    first = group * row_chunk
+                    place = block * row_count + first
+                    low_dist = [lower[0, first + t, 0] for t in range(row_chunk)]
+                    low_coef = [lower[0, first + t, 1] for t in range(row_chunk)]
+                    parts = [jnp.zeros(wide, jnp.float32)] * row_chunk
+                    for v in range(tile_side):
+                        for t in range(row_chunk):
+                            line = weights_back[place + t, v : v + 1, :]
+                            wide_dist = jnp.broadcast_to(low_dist[t][:, v : v + 1], wide)
+                            wide_coef = jnp.broadcast_to(low_coef[t][:, v : v + 1], wide)
+                            parts[t] += jnp.where(upper + line == wide_dist, wide_coef, 0.0)
+                    return total + sum(parts[1:], parts[0])
+
+                sums_out[0, block] = lax.fori_loop(
+                    0, row_count // row_chunk, columns, jnp.zeros(wide, jnp.float32)
+                )
+                return carried
+
+            lax.fori_loop(0, col_count, from_block, 0)
+        else:
+            lax.fori_loop(0, col_count, clear, 0)
+
+            def from_column(step, carried):
+                column = partner(my_row, step, row_count)
+
+                @pl.when(step > 0)
+                def _():
                     arrived("row", LEVELS + back, column, lower.at[back, column, 1])
 
-            low_dist = lower[0, column, 0]
-            low_coef = lower[back, column, 1]
-
-            def blocks(group, carried):
-                first = group * col_chunk
-                upper = [band[last, first + t, 0] for t in range(col_chunk)]
-                total = [sums_out[back, first + t] for t in range(col_chunk)]
-                for v in range(tile_side):
-                    wide_dist = jnp.broadcast_to(low_dist[:, v : v + 1], wide)
-                    wide_coef = jnp.broadcast_to(low_coef[:, v : v + 1], wide)
+                low_dist = lower[0, column, 0]
+                low_coef = lower[back, column, 1]
+
+                def blocks(group, carried):
+                    first = group * col_chunk
+                    upper = [band[last, first + t, 0] for t in range(col_chunk)]
+                    total = [sums_out[back, first + t] for t in range(col_chunk)]
+                    for v in range(tile_side):
+                        wide_dist = jnp.broadcast_to(low_dist[:, v : v + 1], wide)
+                        wide_coef = jnp.broadcast_to(low_coef[:, v : v + 1], wide)
+                        for t in range(col_chunk):
+                            line = weights_back[(first + t) * row_count + column, v : v + 1, :]
+                            total[t] += jnp.where(upper[t] + line == wide_dist, wide_coef, 0.0)
                     for t in range(col_chunk):
-                        line = weights_back[(first + t) * row_count + column, v : v + 1, :]
-                        total[t] += jnp.where(upper[t] + line == wide_dist, wide_coef, 0.0)
-                for t in range(col_chunk):
-                    sums_out[back, first + t] = total[t]
-                return carried
-
-            return lax.fori_loop(0, col_count // col_chunk, blocks, carried)
-
-        lax.fori_loop(0, row_count, from_column, 0)
+                        sums_out[back, first + t] = total[t]
+                    return carried
+
+                return lax.fori_loop(0, col_count // col_chunk, blocks, carried)
+
+            lax.fori_loop(0, row_count, from_column, 0)
         stage = LEVELS + back
         push("col", stage, lambda other: sums_out.at[back, other], sums_in.at[back, my_col])
         summed = sums_out[back, my_col]
@@ -321,11 +347,15 @@
             arrived("col", stage, other, sums_in.at[back, other])
             summed += sums_in[back, other]
         dependency = own_paths * summed
-    cent_out[...] = (
-        jnp.sum(jnp.where(own_source, 0.0, dependency), axis=0, keepdims=True) / source_rows
-    )
+    packed[2] = jnp.where(own_source, 0.0, dependency)
     for copy in pending:
         copy.wait_send()
+
+
+def unpack(packed, dist_out, path_out, cent_out):
+    dist_out[...] = packed[0]
+    path_out[...] = packed[1]
+    cent_out[...] = jnp.sum(packed[2], axis=0, keepdims=True) / packed.shape[1]
 
 
 def solution(mesh):
@@ -340,15 +370,11 @@
         positions = row_count * col_count
         vector = pl.BlockSpec(memory_space=pltpu.VMEM)
         scalar = pl.BlockSpec(memory_space=pltpu.SMEM)
-        distance, paths, centrality = pl.pallas_call(
+        packed = pl.pallas_call(
             functools.partial(body, row_count, col_count),
-            out_shape=(
-                jax.ShapeDtypeStruct(wide, jnp.float32),
-                jax.ShapeDtypeStruct(wide, jnp.float32),
-                jax.ShapeDtypeStruct((1, tile_side), jnp.float32),
-            ),
+            out_shape=jax.ShapeDtypeStruct((3,) + wide, jnp.float32),
             in_specs=[scalar, scalar, scalar, pl.BlockSpec(memory_space=pl.ANY)],
-            out_specs=(vector, vector, vector),
+            out_specs=vector,
             scratch_shapes=[
                 pltpu.VMEM((slot_total, tile_side, tile_side), jnp.float32),
                 pltpu.SMEM((positions,), jnp.int32),
@@ -370,7 +396,17 @@
                 collective_id=0,
                 has_side_effects=True,
             ),
-        )(tile_index, tile_count, sources, tiles)
+        )(tile_index.T, tile_count, sources, tiles)
+        distance, paths, centrality = pl.pallas_call(
+            unpack,
+            out_shape=(
+                jax.ShapeDtypeStruct(wide, jnp.float32),
+                jax.ShapeDtypeStruct(wide, jnp.float32),
+                jax.ShapeDtypeStruct((1, tile_side), jnp.float32),
+            ),
+            in_specs=[vector],
+            out_specs=(vector, vector, vector),
+        )(packed)
         return distance, paths, centrality.reshape(tile_side)
 
     in_specs = (

time: 45 us -> 46.3 us (1.029)
  Pallas kernels: 40.2 us -> 44.7 us
  local copies, waits for them, and re-layouts: 3.16 us -> 0 us
    pallas_call x1 -> x2, Pallas kernels: 40.2 us -> 44.7 us  [the longest x1 43.4 us: per_device(): pl.pallas_call(functools.partial(body, row_count, col_count), out_shape=j...]
    unnamed x12 -> x0, local copies, waits for them, and re-layouts: 3.16 us -> none
where the time goes in v2:
time: 46.3 us; the launch traced here: 46 us
  Pallas kernels  44.7 us (97%)
  between operations  1.29 us (3%)
    pallas_call x1, Pallas kernels, per_device(): pl.pallas_call(functools.partial(body, row_count, col_count), out_shape=j...  43.4 us
    pallas_call x1, Pallas kernels, per_device(): pl.pallas_call(unpack, out_shape=(jax.ShapeDtypeStruct(wide, jnp.float32)...  1.31 us

profile of v2, /device:TPU:0, one launch (start us, length us, event | category | flops | bytes accessed | tf_op | source)
XLA Modules:
  0.0 46.0 jit_solution(8051272493766415872)
XLA Ops:
  1.3 43.4 %shard_map.67.packed = f32[3,8,128]{2,1,0:T(8,128)} custom-call(s32[2,16]{1,0:T(2,128)} %bitcast.2, s32[1]{0:T(128)S(6)} %copy.7.count_ref, s32[8]{0:T(128)} %source_ref.1, f32[16,128,128]{2,1,0:T(8,128)} %tiles_ref.1), custom_call_target="tpu_custom_call" | custom-call | tf_op jit(solution)/shard_map/pallas_call | solution.py:373
  44.7 1.3 %shard_map.68 = (f32[8,128]{1,0:T(8,128)}, f32[8,128]{1,0:T(8,128)}, f32[1,128]{1,0:T(1,128)}) custom-call(f32[3,8,128]{2,1,0:T(8,128)} %shard_map.67.packed), custom_call_target="tpu_custom_call" | custom-call | tf_op jit(solution)/shard_map/pallas_call | solution.py:400

commit v3 on v2

v3 whole, which is shorter than its diff:
```python
import functools

import jax
import jax.numpy as jnp
from jax import lax
from jax.experimental import pallas as pl
from jax.experimental.pallas import tpu as pltpu
from jax.sharding import PartitionSpec as P

LEVELS = 3
BACK = 2
CHUNK = 4

far_value = 1000000.0
no_edge = 2000000.0
half_far = 500000.0


def partner(me, step, count):
    if count & (count - 1):
        return (me + step) % count
    total = 0
    bit = 1
    while bit < count:
        total = total + ((me // bit) % 2 + (step // bit) % 2) % 2 * bit
        bit *= 2
    return total


def body(
    row_count,
    col_count,
    index_ref,
    count_ref,
    source_ref,
    tiles_ref,
    packed,
    raw,
    place_ref,
    weights,
    weights_back,
    partial,
    inbox,
    full,
    band,
    lower,
    sums_out,
    sums_all,
    sums_in,
    load_sem,
    all_send,
    all_recv,
    full_send,
    full_recv,
    col_send,
    col_recv,
):
    slot_total, tile_side = raw.shape[0], raw.shape[1]
    source_rows = source_ref.shape[0]
    my_row = lax.axis_index("row")
    my_col = lax.axis_index("col")
    positions = row_count * col_count
    row_chunk = CHUNK if row_count % CHUNK == 0 else 1
    col_chunk = CHUNK if col_count % CHUNK == 0 else 1
    wide = (source_rows, tile_side)
    pending = []

    def others():
        for col_step in reversed(range(col_count)):
            for row_step in reversed(range(row_count)):
                if row_step or col_step:
                    yield (
                        partner(my_row, row_step, row_count),
                        partner(my_col, col_step, col_count),
                        row_step,
                        col_step,
                    )

    load = pltpu.make_async_copy(tiles_ref, raw, load_sem)
    load.start()
    barrier = pltpu.get_barrier_semaphore()
    for other_row, other_col, _, _ in others():
        pl.semaphore_signal(
            barrier,
            inc=1,
            device_id={"row": other_row, "col": other_col},
            device_id_type=pl.DeviceIdType.MESH,
        )

    def start(source, target, send, recv, device):
        copy = pltpu.make_async_remote_copy(
            src_ref=source,
            dst_ref=target,
            send_sem=send,
            recv_sem=recv,
            device_id=device,
            device_id_type=pl.DeviceIdType.MESH,
        )
        copy.start()
        pending.append(copy)

    def push_all(stage, source_of, target):
        for other_row, other_col, row_step, col_step in others():
            start(
                source_of(other_row, other_col),
                target,
                all_send.at[stage, row_step, col_step],
                all_recv.at[stage, my_row, my_col],
                {"row": other_row, "col": other_col},
            )

    def arrived(target, recv, device):
        pltpu.make_async_remote_copy(
            src_ref=target,
            dst_ref=target,
            send_sem=load_sem,
            recv_sem=recv,
            device_id=device,
            device_id_type=pl.DeviceIdType.MESH,
        ).wait_recv()

    def source_mask(base):
        wanted = jnp.full(wide, -1, jnp.int32)
        for row in range(source_rows):
            wanted = jnp.where(sub == row, source_ref[row] - base, wanted)
        return lane == wanted

    def settle(found_dist, found_count, is_source):
        start_dist = jnp.where(is_source, 0.0, far_value).astype(jnp.float32)
        settled = jnp.minimum(start_dist, found_dist)
        ones = jnp.where(is_source, 1.0, 0.0).astype(jnp.float32)
        return settled, ones + jnp.where(found_dist == settled, found_count, 0.0)

    def combine(pieces):
        best, total = pieces[0]
        for other_best, other_total in pieces[1:]:
            both = jnp.minimum(best, other_best)
            total = jnp.where(best == both, total, 0.0) + jnp.where(
                other_best == both, other_total, 0.0
            )
            best = both
        return best, total

    live_count = count_ref[0]
    holds = []
    for slot in range(slot_total):
        position = index_ref[0, slot] * row_count + index_ref[1, slot]
        holds.append(jnp.where(slot < live_count, position, -1))

    def find_slot(position, carried):
        found = jnp.int32(-1)
        for slot in range(slot_total):
            found = jnp.where(holds[slot] == position, jnp.int32(slot), found)
        place_ref[position] = found
        return carried

    lax.fori_loop(0, positions, find_slot, 0)

    lane = lax.broadcasted_iota(jnp.int32, wide, 1)
    sub = lax.broadcasted_iota(jnp.int32, wide, 0)
    load.wait()

    band_base = my_row * col_count * tile_side

    def first_level(column, carried):
        best = jnp.full(wide, far_value, jnp.float32)
        for row in range(source_rows):
            place = source_ref[row] - band_base
            inside = (place >= 0) & (place < col_count * tile_side)
            place = jnp.clip(place, 0, col_count * tile_side - 1)
            slot = place_ref[(place // tile_side) * row_count + column]
            line = raw[jnp.maximum(slot, 0), pl.ds(place % tile_side, 1), :]
            limit = jnp.where(inside & (slot >= 0), 0.0, far_value).astype(jnp.float32)
            best = jnp.where((sub == row) & (line > limit), line, best)
        partial[0, column, 0] = best
        return carried

    lax.fori_loop(0, row_count, first_level, 0)
    inbox[0, my_col, my_row, 0] = partial[0, my_row, 0]
    pl.semaphore_wait(barrier, row_count * col_count - 1)
    push_all(
        0, lambda other_row, other_col: partial.at[0, other_row, 0], inbox.at[0, my_col, my_row, 0]
    )

    def prepare(position, carried):
        slot = place_ref[position]
        tile = raw[jnp.maximum(slot, 0)]
        limit = jnp.where(slot >= 0, 0.0, far_value).astype(jnp.float32)
        weights[position] = jnp.where(tile > limit, tile, no_edge)
        return carried

    lax.fori_loop(0, positions, prepare, 0)

    def turn(position, carried):
        weights_back[position] = weights[position].T
        return carried

    def band_block(stage, block, step):
        for row_step in range(row_count):
            giver = partner(my_row, row_step, row_count)

            def wait():
                piece = inbox.at[stage, block, giver]
                arrived(
                    piece.at[0] if stage in (0, LEVELS - 1) else piece,
                    all_recv.at[stage, giver, block],
                    {"row": giver, "col": block},
                )

            if row_step == 0:
                pl.when(step > 0)(wait)
            else:
                wait()
        is_source = source_mask((my_row * col_count + block) * tile_side)
        if stage in (0, LEVELS - 1):
            best = inbox[stage, block, 0, 0]
            for giver in range(1, row_count):
                best = jnp.minimum(best, inbox[stage, block, giver, 0])
            best = jnp.where(is_source, 0.0, best)
            return best, jnp.where(best < half_far, 1.0, 0.0).astype(jnp.float32)
        found = combine([(inbox[stage, block, g, 0], inbox[stage, block, g, 1]) for g in range(row_count)])
        return settle(*found, is_source)

    def forward(level):
        best_ref = partial.at[level]

        def clear(column, carried):
            best_ref[column, 0] = jnp.full(wide, far_value, jnp.float32)
            best_ref[column, 1] = jnp.zeros(wide, jnp.float32)
            return carried

        lax.fori_loop(0, row_count, clear, 0)

        def from_block(step, carried):
            block = partner(my_col, step, col_count)

            near_dist, near_count = band_block(level - 1, block, step)

            def columns(group, carried):
                first = group * row_chunk
                place = block * row_count + first
                before = [best_ref[first + t, 0] for t in range(row_chunk)]
                best = list(before)
                for u in range(tile_side):
                    wide_dist = jnp.broadcast_to(near_dist[:, u : u + 1], wide)
                    for t in range(row_chunk):
                        line = weights[place + t, u : u + 1, :]
                        best[t] = jnp.minimum(best[t], wide_dist + line)
                total = [
                    jnp.where(before[t] == best[t], best_ref[first + t, 1], 0.0)
                    for t in range(row_chunk)
                ]
                for u in range(tile_side):
                    wide_dist = jnp.broadcast_to(near_dist[:, u : u + 1], wide)
                    wide_count = jnp.broadcast_to(near_count[:, u : u + 1], wide)
                    for t in range(row_chunk):
                        line = weights[place + t, u : u + 1, :]
                        total[t] += jnp.where(wide_dist + line == best[t], wide_count, 0.0)
                for t in range(row_chunk):
                    best_ref[first + t, 0] = best[t]
                    best_ref[first + t, 1] = total[t]
                return carried

            return lax.fori_loop(0, row_count // row_chunk, columns, carried)

        lax.fori_loop(0, col_count, from_block, 0)
        inbox[level, my_col, my_row] = best_ref[my_row]
        if level == LEVELS - 1:
            push_all(
                level,
                lambda other_row, other_col: best_ref.at[other_row, 0],
                inbox.at[level, my_col, my_row, 0],
            )
        else:
            push_all(
                level,
                lambda other_row, other_col: best_ref.at[other_row],
                inbox.at[level, my_col, my_row],
            )

    lax.fori_loop(0, positions, turn, 0)
    for level in range(1, LEVELS):
        forward(level)

    last = LEVELS - 1
    full[my_row] = partial[last]
    for row_step in reversed(range(1, row_count)):
        other = partner(my_row, row_step, row_count)
        start(
            partial.at[last],
            full.at[my_row],
            full_send.at[row_step],
            full_recv.at[my_row],
            {"row": other, "col": my_col},
        )
    for row_step in range(1, row_count):
        other = partner(my_row, row_step, row_count)
        arrived(full.at[other], full_recv.at[other], {"row": other, "col": my_col})

    def settle_column(column, carried):
        found = combine([(full[g, column, 0], full[g, column, 1]) for g in range(row_count)])
        base = (column * col_count + my_col) * tile_side
        lower[0, column], lower[1, column] = settle(*found, source_mask(base))
        return carried

    lax.fori_loop(0, row_count, settle_column, 0)
    own_dist = lower[0, my_row]
    own_paths = lower[1, my_row]
    packed[0] = jnp.where(own_dist < half_far, own_dist, -1.0)
    packed[1] = own_paths

    def settle_block(step, carried):
        block = partner(my_col, step, col_count)
        band[block] = band_block(last, block, step)[0]
        return carried

    lax.fori_loop(0, col_count, settle_block, 0)

    for back in range(BACK):

        def clear(block, carried):
            sums_out[back, block] = jnp.zeros(wide, jnp.float32)
            return carried

        lax.fori_loop(0, col_count, clear, 0)

        def from_column(step, carried):
            column = partner(my_row, step, row_count)
            low_dist = lower[0, column]
            low_paths = lower[1, column]
            if back == 0:
                dependency = 0.0
            else:
                summed = jnp.zeros(wide, jnp.float32)
                for col_step in range(col_count):
                    giver = partner(my_col, col_step, col_count)

                    def wait():
                        arrived(
                            sums_all.at[column, giver],
                            all_recv.at[LEVELS, column, giver],
                            {"row": column, "col": giver},
                        )

                    if col_step == 0:
                        pl.when(step > 0)(wait)
                    else:
                        wait()
                for giver in range(col_count):
                    summed += sums_all[column, giver]
                dependency = low_paths * summed
            low_coef = jnp.where(
                low_paths > 0.5, (1.0 + dependency) / jnp.maximum(low_paths, 1.0), 0.0
            )

            def blocks(group, carried):
                first = group * col_chunk
                upper = [band[first + t] for t in range(col_chunk)]
                total = [sums_out[back, first + t] for t in range(col_chunk)]
                for v in range(tile_side):
                    wide_dist = jnp.broadcast_to(low_dist[:, v : v + 1], wide)
                    wide_coef = jnp.broadcast_to(low_coef[:, v : v + 1], wide)
                    for t in range(col_chunk):
                        line = weights_back[(first + t) * row_count + column, v : v + 1, :]
                        total[t] += jnp.where(upper[t] + line == wide_dist, wide_coef, 0.0)
                for t in range(col_chunk):
                    sums_out[back, first + t] = total[t]
                return carried

            return lax.fori_loop(0, col_count // col_chunk, blocks, carried)

        lax.fori_loop(0, row_count, from_column, 0)
        if back == 0:
            sums_all[my_row, my_col] = sums_out[0, my_col]
            push_all(
                LEVELS,
                lambda other_row, other_col: sums_out.at[0, other_col],
                sums_all.at[my_row, my_col],
            )
    for col_step in reversed(range(1, col_count)):
        other = partner(my_col, col_step, col_count)
        start(
            sums_out.at[1, other],
            sums_in.at[my_col],
            col_send.at[col_step],
            col_recv.at[my_col],
            {"row": my_row, "col": other},
        )
    summed = sums_out[1, my_col]
    for col_step in range(1, col_count):
        other = partner(my_col, col_step, col_count)
        arrived(sums_in.at[other], col_recv.at[other], {"row": my_row, "col": other})
        summed += sums_in[other]
    own_source = source_mask((my_row * col_count + my_col) * tile_side)
    packed[2] = jnp.where(own_source, 0.0, own_paths * summed)
    for copy in pending:
        copy.wait_send()


def unpack(packed, dist_out, path_out, cent_out):
    dist_out[...] = packed[0]
    path_out[...] = packed[1]
    cent_out[...] = jnp.sum(packed[2], axis=0, keepdims=True) / packed.shape[1]


def solution(mesh):
    row_count = mesh.shape["row"]
    col_count = mesh.shape["col"]

    def per_device(tiles, tile_index, tile_count, sources):
        slot_total, tile_side = tiles.shape[0], tiles.shape[1]
        source_rows = sources.shape[0]
        wide = (source_rows, tile_side)
        positions = row_count * col_count
        vector = pl.BlockSpec(memory_space=pltpu.VMEM)
        scalar = pl.BlockSpec(memory_space=pltpu.SMEM)
        packed = pl.pallas_call(
            functools.partial(body, row_count, col_count),
            out_shape=jax.ShapeDtypeStruct((3,) + wide, jnp.float32),
            in_specs=[scalar, scalar, scalar, pl.BlockSpec(memory_space=pl.ANY)],
            out_specs=vector,
            scratch_shapes=[
                pltpu.VMEM((slot_total, tile_side, tile_side), jnp.float32),
                pltpu.SMEM((positions,), jnp.int32),
                pltpu.VMEM((positions, tile_side, tile_side), jnp.float32),
                pltpu.VMEM((positions, tile_side, tile_side), jnp.float32),
                pltpu.VMEM((LEVELS, row_count, 2) + wide, jnp.float32),
                pltpu.VMEM((LEVELS, col_count, row_count, 2) + wide, jnp.float32),
                pltpu.VMEM((row_count, row_count, 2) + wide, jnp.float32),
                pltpu.VMEM((col_count,) + wide, jnp.float32),
                pltpu.VMEM((2, row_count) + wide, jnp.float32),
                pltpu.VMEM((BACK, col_count) + wide, jnp.float32),
                pltpu.VMEM((row_count, col_count) + wide, jnp.float32),
                pltpu.VMEM((col_count,) + wide, jnp.float32),
                pltpu.SemaphoreType.DMA,
                pltpu.SemaphoreType.DMA((LEVELS + 1, row_count, col_count)),
                pltpu.SemaphoreType.DMA((LEVELS + 1, row_count, col_count)),
                pltpu.SemaphoreType.DMA((row_count,)),
                pltpu.SemaphoreType.DMA((row_count,)),
                pltpu.SemaphoreType.DMA((col_count,)),
                pltpu.SemaphoreType.DMA((col_count,)),
            ],
            compiler_params=pltpu.CompilerParams(
                collective_id=0,
                has_side_effects=True,
            ),
        )(tile_index.T, tile_count, sources, tiles)
        distance, paths, centrality = pl.pallas_call(
            unpack,
            out_shape=(
                jax.ShapeDtypeStruct(wide, jnp.float32),
                jax.ShapeDtypeStruct(wide, jnp.float32),
                jax.ShapeDtypeStruct((1, tile_side), jnp.float32),
            ),
            in_specs=[vector],
            out_specs=(vector, vector, vector),
        )(packed)
        return distance, paths, centrality.reshape(tile_side)

    in_specs = (
        P(("groups", "row", "col"), None, None),
        P(("groups", "row", "col"), None),
        P(("groups", "row", "col")),
        P("groups"),
    )
    out_specs = (
        P("groups", ("row", "col")),
        P("groups", ("row", "col")),
        P(("groups", "row", "col")),
    )
    return jax.shard_map(
        per_device, mesh=mesh, in_specs=in_specs, out_specs=out_specs, check_vma=False
    )
```

time: 46.3 us -> 38.5 us (0.83)
  Pallas kernels: 44.7 us -> 36.9 us
    pallas_call x1, Pallas kernels: 43.4 us -> 35.6 us  [per_device(): pl.pallas_call(functools.partial(body, row_count, col_count), out_shape=j...]
where the time goes in v3:
time: 38.5 us; the launch traced here: 38.2 us
  Pallas kernels  36.9 us (96%)
  between operations  1.29 us (3%)
    pallas_call x1, Pallas kernels, per_device(): pl.pallas_call(functools.partial(body, row_count, col_count), out_shape=j...  35.6 us
    pallas_call x1, Pallas kernels, per_device(): pl.pallas_call(unpack, out_shape=(jax.ShapeDtypeStruct(wide, jnp.float32)...  1.31 us

profile of v3, /device:TPU:0, one launch (start us, length us, event | category | flops | bytes accessed | tf_op | source)
XLA Modules:
  0.0 38.2 jit_solution(8678876949429006133)
XLA Ops:
  1.3 35.6 %shard_map.67.packed = f32[3,8,128]{2,1,0:T(8,128)} custom-call(s32[2,16]{1,0:T(2,128)} %bitcast.2, s32[1]{0:T(128)S(6)} %copy.7.count_ref, s32[8]{0:T(128)} %source_ref.1, f32[16,128,128]{2,1,0:T(8,128)} %tiles_ref.1), custom_call_target="tpu_custom_call" | custom-call | tf_op jit(solution)/shard_map/pallas_call | solution.py:417
  36.9 1.3 %shard_map.68 = (f32[8,128]{1,0:T(8,128)}, f32[8,128]{1,0:T(8,128)}, f32[1,128]{1,0:T(1,128)}) custom-call(f32[3,8,128]{2,1,0:T(8,128)} %shard_map.67.packed), custom_call_target="tpu_custom_call" | custom-call | tf_op jit(solution)/shard_map/pallas_call | solution.py:448
